TPU v7x, 128 devices: a whole 4x4x4 slice. The times are simulated.
128 devices in a mesh: ctx: 16 (over y, x_lo, core), head: 8 (over z, x_hi).
Axes of the slice: x: 4 (x_hi: 2, x_lo: 2; x = x_hi * 2 + x_lo), y: 4, z: 4, core: 2. Of those that a mesh axis runs over, the one named last changes fastest.
Arguments:
- q_prompt: bfloat16 [8192, 32, 256], P('ctx', 'head'), may hold values from -0.3984375 to 0.3984375
- k_prompt: bfloat16 [8192, 32, 256], P('ctx', 'head'), may hold values from -0.3984375 to 0.3984375
- v_prompt: bfloat16 [8192, 32, 256], P('ctx', 'head'), may hold values from -6 to 6
- log_decay: float32 [32, 8192], P('head', 'ctx'), may hold values from -1 to 0
- prompt_section: int32 [512, 1], P('ctx'), may hold values from 0 to 15; in each aligned block of 32 rows (0 to 31, 32 to 63, ...) at most 4 rows name the same one
- q_step: bfloat16 [512, 4, 32, 256], P('ctx', None, 'head'), may hold values from -0.3984375 to 0.3984375
- k_step: bfloat16 [512, 4, 32, 256], P('ctx', None, 'head'), may hold values from -3 to 3
- v_step: bfloat16 [512, 4, 32, 256], P('ctx', None, 'head'), may hold values from -6 to 6
- step_decay: float32 [32, 4, 512], P('head', None, 'ctx'), may hold values from -0.6 to -0.05
- w_out: bfloat16 [8192, 8192], P(None, 'head'), may hold values from -0.0625 to 0.0625
Outputs:
- prompt_out: bfloat16 [8192, 8192], P('ctx', 'head')
- step_out: bfloat16 [512, 4, 8192], P('ctx', None, 'head')
Inputs may be any that keep to these rules, and one draw needn't show every extreme that they name: `prompt_section`: among the rows of one index of ctx, no section is named more than 4 times.
All inputs are finite; a program needn't handle non-finite values.
Results may differ from a plain program's by a relative error of at most 0.015.
Values may be sent and summed in bfloat16 or wider, within the bound.
No kernel may reach another device: no remote copies, remote signals or barrier semaphores. Data moves between devices by JAX's collectives and lax.ppermute only.
A program may use at most 128 MiB of HBM per device.

v0:
```python
import jax
import jax.numpy as jnp
from jax import lax
from jax.sharding import PartitionSpec as P

CAP = 4


def entering(value, axis, join, neutral):
    count, mine = (lax.axis_size(axis), lax.axis_index(axis))
    pieces = jax.tree.map(lambda part: lax.all_gather(part, axis), value)
    running = jax.tree.map(
        lambda part, zero: jnp.full_like(part, 0) + jnp.asarray(zero, part.dtype), value, neutral
    )

    def step(position, running):
        longer = join(running, jax.tree.map(lambda part: part[position], pieces))
        return jax.tree.map(lambda new, old: jnp.where(position < mine, new, old), longer, running)

    return lax.fori_loop(0, count - 1, step, running)


def as_sent(value):
    return jax.tree.map(lambda a: a.astype(jnp.bfloat16) if a.dtype == jnp.float32 else a, value)


def split_state(state):
    high_part = state.astype(jnp.bfloat16)
    rest = state - lax.optimization_barrier(high_part).astype(jnp.float32)
    middle_part = rest.astype(jnp.bfloat16)
    low_part = (rest - lax.optimization_barrier(middle_part).astype(jnp.float32)).astype(
        jnp.bfloat16
    )
    return (high_part, middle_part, low_part)


def exact_read(form, query_rows, state):
    parts = split_state(state)
    total = jnp.einsum(form, query_rows, parts[0], preferred_element_type=jnp.float32)
    total = total + jnp.einsum(form, query_rows, parts[1], preferred_element_type=jnp.float32)
    return total + jnp.einsum(form, query_rows, parts[2], preferred_element_type=jnp.float32)


def block_terms(carry_state, query_rows, key_matrix_rows, value_rows, log_rates):
    positions = jnp.arange(log_rates.shape[1])
    causal = positions[:, None] >= positions[None, :]
    cumlog = jnp.cumsum(log_rates, axis=1)
    decays = jnp.where(
        causal[None], jnp.exp(jnp.minimum(cumlog[:, :, None] - cumlog[:, None, :], 0.0)), 0.0
    )
    attention_scores = jnp.einsum(
        "jsv,csv->sjc", query_rows, key_matrix_rows, preferred_element_type=jnp.float32
    )
    weights = (attention_scores * decays).astype(jnp.bfloat16)
    within = jnp.einsum("hnm,mhe->nhe", weights, value_rows, preferred_element_type=jnp.float32)
    carried = exact_read("nhd,hde->nhe", query_rows, carry_state)
    carried = carried * jnp.exp(cumlog).T[:, :, None]
    last_log = cumlog[:, -1]
    weighted_values = (
        key_matrix_rows.astype(jnp.float32) * jnp.exp(last_log[:, None] - cumlog).T[:, :, None]
    ).astype(jnp.bfloat16)
    state_update = jnp.einsum(
        "jxa,jxp->xap", weighted_values, value_rows, preferred_element_type=jnp.float32
    )
    carry_state = jnp.exp(last_log)[:, None, None] * carry_state + state_update
    return (carry_state, within + carried, cumlog)


def combine(earlier, latter):
    return (earlier[0] + latter[0], jnp.exp(latter[0])[:, None, None] * earlier[1] + latter[1])


def shards(
    q_prompt,
    k_prompt,
    v_prompt,
    log_decay,
    prompt_section,
    q_step,
    k_step,
    v_step,
    step_decay,
    w_out,
):
    token_count, heads_here, head_dim = q_prompt.shape
    sections = lax.axis_size("ctx")
    carry_state = jnp.zeros((heads_here, head_dim, head_dim), jnp.float32)
    carry_state, partial_value, cumlog = block_terms(
        carry_state, q_prompt, k_prompt, v_prompt, log_decay
    )
    offset = cumlog[:, -1]
    identity = (jnp.zeros_like(offset), jnp.zeros_like(carry_state))
    earlier_log, entry_state = entering((offset, carry_state), "ctx", combine, identity)
    entry_parts = split_state(entry_state)
    entry_read = jnp.einsum(
        "nhd,hde->nhe", q_prompt, entry_parts[0], preferred_element_type=jnp.float32
    )
    entry_read = entry_read + jnp.einsum(
        "nhd,hde->nhe", q_prompt, entry_parts[1], preferred_element_type=jnp.float32
    )
    entry_read = entry_read + jnp.einsum(
        "nhd,hde->nhe", q_prompt, entry_parts[2], preferred_element_type=jnp.float32
    )
    block_out = partial_value + jnp.exp(cumlog).T[:, :, None] * entry_read
    retained = block_out.astype(jnp.bfloat16)
    retention = retained.reshape(token_count, heads_here * head_dim)

    def project_into(shard_piece):
        return jnp.dot(shard_piece, w_out, preferred_element_type=jnp.float32)

    prompt_out = project_into(lax.all_gather(retention, "head", axis=1, tiled=True))
    prompt_out = prompt_out.astype(jnp.bfloat16)
    final_state = jnp.exp(offset)[:, None, None] * entry_state + carry_state
    row_count, step_count = (q_step.shape[0], q_step.shape[1])
    section_ids = prompt_section[:, 0]
    owner_hot = (section_ids[:, None] == jnp.arange(sections)[None, :]).astype(jnp.float32)
    before = jnp.tril(jnp.ones((row_count, row_count), jnp.float32), -1)
    counts_before = jnp.dot(before, owner_hot, precision=lax.Precision.HIGHEST)
    ranking = jnp.sum(counts_before * owner_hot, axis=1).astype(jnp.int32)
    slot_ids = section_ids * CAP + ranking
    selector = (jnp.arange(sections * CAP)[:, None] == slot_ids[None, :]).astype(jnp.bfloat16)
    packed = jnp.dot(selector, q_step.reshape(row_count, -1), preferred_element_type=jnp.float32)
    packed = packed.astype(jnp.bfloat16).reshape(sections, CAP, step_count, heads_here, head_dim)
    reads = exact_read(
        "jcthd,jhde->jcthe",
        packed,
        lax.all_gather(as_sent(final_state[None]), "ctx", axis=0, tiled=True),
    )
    slot_reads = reads
    slot_reads = slot_reads.reshape(sections * CAP, step_count, heads_here, head_dim)
    prefix_reads = jnp.take(slot_reads, slot_ids, axis=0)
    step_logs = jnp.cumsum(jnp.transpose(step_decay, (2, 1, 0)), axis=1)
    head_logs = jnp.transpose(step_logs, (0, 2, 1))
    step_index = jnp.arange(step_count)
    causal = step_index[:, None] >= step_index[None, :]
    step_weights = jnp.where(
        causal[None, None],
        jnp.exp(jnp.minimum(head_logs[:, :, :, None] - head_logs[:, :, None, :], 0.0)),
        0.0,
    )
    attention_scores = jnp.einsum(
        "rthd,ruhd->rhtu", q_step, k_step, preferred_element_type=jnp.float32
    )
    own_terms = jnp.einsum(
        "rhtu,ruhe->rthe", attention_scores * step_weights, v_step.astype(jnp.float32)
    )
    step_retention = (jnp.exp(step_logs)[:, :, :, None] * prefix_reads + own_terms).astype(
        jnp.bfloat16
    )
    step_flat = step_retention.reshape(row_count * step_count, heads_here * head_dim)
    step_out = project_into(lax.all_gather(step_flat, "head", axis=1, tiled=True))
    step_out = step_out.astype(jnp.bfloat16).reshape(row_count, step_count, w_out.shape[1])
    return (prompt_out, step_out)


def solution(mesh):
    in_specs = (
        P("ctx", "head", None),
        P("ctx", "head", None),
        P("ctx", "head", None),
        P("head", "ctx"),
        P("ctx", None),
        P("ctx", None, "head", None),
        P("ctx", None, "head", None),
        P("ctx", None, "head", None),
        P("head", None, "ctx"),
        P(None, "head"),
    )
    out_specs = (P("ctx", "head"), P("ctx", None, "head"))
    return jax.shard_map(shards, mesh=mesh, in_specs=in_specs, out_specs=out_specs, check_vma=False)
```

profile of v0, /device:TPU:1, one launch (start us, length us, event | category | flops | bytes accessed | tf_op | source)
XLA Modules:
  0.0 372.0 jit_solution(12672800232312546022)
XLA Ops:
  7.2 0.8 reshape.123
  8.0 1.2 reduce-window.6
  9.2 0.2 slice_reduce_fusion
  9.4 0.2 reduce-window.9
  9.7 0.1 copy.91
  9.9 0.2 copy.64
  10.1 1.8 multiply_convert_fusion.1
  11.8 1.2 dynamic-slice
  13.7 0.1 bitcast_exponential_fusion
  13.8 1.5 convolution_add_fusion
  15.5 28.4 %all-reduce = f32[64]{0:T(128)S(1)} all-reduce(f32[64]{0:T(128)S(1)} %get-tuple-element.133), channel_id=2, replica_groups=mesh['ctx'=16,'head'=8] {'ctx'}, use_global_device_ids=true, to_apply=%add | all-reduce | flops 64 | bytes 512
  43.9 0.1 reshape.139
  44.0 66.9 %all-gather.12.cloned.1.call-done = f32[64,256,256]{2,1,0:T(8,128)} async-done(((f32[4,256,256]{2,1,0:T(8,128)}), f32[64,256,256]{2,1,0:T(8,128)}) %all-gather.12.cloned.1.call-update) | async-done | bytes 16777232 | tf_op jit(solution)/shard_map/all_gather | solution.py:11
  110.9 24.1 %while.14 = (s32[]{:T(128)}, f32[4,256,256]{2,1,0:T(8,128)S(1)}, s32[]{:T(128)}, f32[16,4]{1,0:T(8,128)S(1)}, f32[16,4,256,256]{3,2,1,0:T(8,128)}, /*index=5*/s32[]{:T(128)}, s32[]{:T(128)}) while((s32[]{:T(128)}, f32[4,256,256]{2,1,0:T(8,128)S(1)}, s32[]{:T(128)}, f32[16,4]{1,0:T(8,128)S(1)}, f32[16,4,256,256]{3,2,1,0:T(8,128)}, ...), condition=%wide.region_3.4_spmd.clone, body=%wide.region_2.3_spmd.clone.sunk | while | flops 1048580 | bytes 3145881 | solution.py:20
  110.9 1.6 fusion.85
  112.5 1.6 fusion.85
  114.1 1.6 fusion.85
  115.7 1.6 fusion.85
  117.4 1.6 fusion.85
  119.0 1.6 fusion.85
  120.6 1.6 fusion.85
  122.2 1.6 fusion.85
  123.8 1.6 fusion.85
  125.4 1.6 fusion.85
  127.0 1.6 fusion.85
  128.6 1.6 fusion.85
  130.2 1.6 fusion.85
  131.8 1.6 fusion.85
  133.5 1.6 fusion.85
  135.0 2.5 add_convert_fusion
  137.7 0.1 fusion.26
  137.9 1.8 fusion.41
  139.7 1.8 fusion.39
  141.5 1.8 fusion.30
  143.3 4.6 %fusion.10 = f32[4,512,256]{1,2,0:T(8,128)} fusion(f32[4,512]{1,0:T(4,128)S(1)} %bitcast.109, pred[512,512]{1,0:T(8,128)(4,1)S(1)} %iota_compare_fusion, bf16[512,4,256]{2,1,0:T(4,128)(2,1)} %param.13, bf16[512,4,256]{2,1,0:T(4,128)(2,1)S(1)} %copy-done, bf16[512,4,256]{2,1,0:T(4,128)(2,1)S(1)} %copy-done.2), kind=kOutput, calls=%fused_computation.20 | convolution fusion | flops 1078984704 | bytes 5513216 | tf_op jit(solution)/shard_map/hnm,mhe->nhe/dot_general | solution.py:55
  147.9 1.3 fusion.29
  149.3 0.5 fusion.34
  149.8 0.5 fusion.36
  150.3 0.7 copy-done.3
  151.0 0.6 copy-done.4
  151.6 0.6 copy-done.5
  152.2 2.1 fusion.8
  154.4 0.2 all-gather.10.cloned.1.call-start
  154.6 0.2 reshape.126
  154.8 0.2 fusion.22
  155.1 0.3 convolution_convert_fusion
  155.3 0.4 reshape.127
  155.8 0.1 copy.73
  155.9 0.1 copy.81
  156.0 34.7 %all-gather.14.cloned.1.call-done = bf16[64,256,256]{2,1,0:T(8,128)(2,1)} async-done(((bf16[4,256,256]{2,1,0:T(8,128)(2,1)}), bf16[64,256,256]{2,1,0:T(8,128)(2,1)}) %all-gather.14.cloned.1.call-update) | async-done | bytes 8388624 | tf_op jit(solution)/shard_map/all_gather | solution.py:127
  190.7 12.6 %fusion.1 = bf16[16,4,256,256]{3,2,1,0:T(8,128)(2,1)} fusion(bf16[16,4,256,256]{3,2,1,0:T(8,128)(2,1)} %bitcast.99), kind=kLoop, calls=%fused_computation.6 | loop fusion | flops 16777216 | bytes 16777216 | tf_op jit(solution)/shard_map/convert_element_type | solution.py:30
  203.4 6.6 %fusion.47 = f32[16,4,256,4,4]{2,4,3,1,0:T(4,128)} fusion(bf16[16,4,256,256,1]{3,2,4,1,0:T(8,128)(2,1)} %bitcast.100, bf16[16,4,4,4,256]{4,3,2,1,0:T(4,128)(2,1)S(1)} %reshape.127), kind=kOutput, calls=%fused_computation.61 | convolution fusion | flops 134217728 | bytes 9961472 | tf_op jit(solution)/shard_map/jcthd,jhde->jcthe/dot_general | solution.py:39
  210.0 12.5 %fusion.5 = f32[16,4,256,4,4]{2,4,3,1,0:T(4,128)} fusion(bf16[16,4,256,256]{3,2,1,0:T(8,128)(2,1)} %fusion.1, bf16[16,4,256,256]{3,2,1,0:T(8,128)(2,1)} %bitcast.101, bf16[16,4,4,4,256]{4,3,2,1,0:T(4,128)(2,1)S(1)} %reshape.127), kind=kOutput, calls=%fused_computation.10 | convolution fusion | flops 159383552 | bytes 18350080 | tf_op jit(solution)/shard_map/jcthd,jhde->jcthe/dot_general | solution.py:41
  222.5 5.3 %fusion.17 = f32[16,4,4,4,256]{4,2,1,3,0:T(4,128)S(1)} fusion(f32[16,4,256,4,4]{2,4,3,1,0:T(4,128)} %fusion.5, f32[16,4,256,4,4]{2,4,3,1,0:T(4,128)} %fusion.47, bf16[16,4,256,256]{3,2,1,0:T(8,128)(2,1)} %fusion.1, bf16[16,4,4,4,256]{4,3,2,1,0:T(4,128)(2,1)S(1)} %reshape.127), kind=kOutput, calls=%fused_computation.24 | convolution fusion | flops 134742016 | bytes 12058624 | tf_op jit(solution)/shard_map/jcthd,jhde->jcthe/dot_general | solution.py:40
  227.7 0.7 copy.77
  228.5 0.9 gather_fusion
  229.3 0.5 fusion.21
  229.9 0.1 copy.84
  230.0 0.7 copy.93
  230.8 70.3 %all-gather.8.cloned.1.call-done = bf16[512,8192]{0,1:T(8,128)(2,1)} async-done(((bf16[512,1024]{0,1:T(8,128)(2,1)}), bf16[512,8192]{0,1:T(8,128)(2,1)}) %all-gather.8.cloned.1.call-update) | async-done | bytes 8388624 | tf_op jit(solution)/shard_map/all_gather | solution.py:111
  301.1 15.6 %convolution_convert_fusion.1 = bf16[512,1024]{1,0:T(8,128)(2,1)} fusion(bf16[512,8192]{0,1:T(8,128)(2,1)} %all-gather.8.cloned.1.call-done, bf16[8192,1024]{1,0:T(8,128)(2,1)} %param.21), kind=kOutput, calls=%fused_computation.19 | convolution fusion | flops 8590458880 | bytes 26214400 | tf_op jit(solution)/shard_map/dot_general | solution.py:109
  316.7 39.1 %all-gather.10.cloned.1.call-done = bf16[128,8192]{1,0:T(8,128)(2,1)} async-done(((bf16[128,1024]{1,0:T(8,128)(2,1)}), bf16[128,8192]{1,0:T(8,128)(2,1)}) %all-gather.10.cloned.1.call-update) | async-done | bytes 2097168 | tf_op jit(solution)/shard_map/all_gather | solution.py:151
  355.8 8.8 %convolution_convert_fusion.2 = bf16[128,1024]{1,0:T(8,128)(2,1)S(1)} fusion(bf16[128,8192]{1,0:T(8,128)(2,1)} %all-gather.10.cloned.1.call-done, bf16[8192,1024]{1,0:T(8,128)(2,1)} %param.21), kind=kOutput, calls=%fused_computation.28 | convolution fusion | flops 2147614720 | bytes 19136512 | tf_op jit(solution)/shard_map/dot_general | solution.py:109
  364.6 0.8 reshape.130
  (60 shorter events, 0.9 us)
Async XLA Ops:
  7.2 6.7 %copy-start = (bf16[512,4,256]{2,1,0:T(4,128)(2,1)S(1)}, bf16[512,4,256]{2,1,0:T(4,128)(2,1)}, u32[]{:S(2)}) copy-start(bf16[512,4,256]{2,1,0:T(4,128)(2,1)} %param.14) | copy-start | bytes 3145732
  7.2 103.7 %all-gather.12.cloned.1.call-start = ((), (), s32[]{:S(2)}) async-start(), calls=%async_computation.2 | async-start | bytes 17825792 | tf_op jit(solution)/shard_map/all_gather | solution.py:11
  15.4 175.3 %all-gather.14.cloned.1.call-start = ((), (), s32[]{:S(2)}) async-start(), calls=%async_computation.3 | async-start | bytes 8912896 | tf_op jit(solution)/shard_map/all_gather | solution.py:127
  135.0 2.8 copy-start.2
  137.6 163.5 %all-gather.8.cloned.1.call-start = ((), (), s32[]{:S(2)}) async-start(), calls=%async_computation | async-start | bytes 9437184 | tf_op jit(solution)/shard_map/all_gather | solution.py:111
  147.9 1.9 copy-start.6
  147.9 2.4 copy-start.7
  149.2 1.7 copy-start.3
  149.2 2.4 copy-start.4
  149.3 3.0 copy-start.5
  152.2 2.4 copy-start.8
  152.2 2.6 copy-start.10
  152.2 3.5 copy-start.9
  154.4 201.4 %all-gather.10.cloned.1.call-start = ((), (), s32[]{:S(2)}) async-start(), calls=%async_computation.1 | async-start | bytes 2359296 | tf_op jit(solution)/shard_map/all_gather | solution.py:151
  222.5 6.9 %copy-start.11 = (bf16[32,4,4,256]{3,2,1,0:T(4,128)(2,1)S(1)}, bf16[32,4,4,256]{3,2,1,0:T(4,128)(2,1)}, u32[]{:S(2)}) copy-start(bf16[32,4,4,256]{3,2,1,0:T(4,128)(2,1)} %param.19) | copy-start | bytes 786436
  222.5 6.9 %copy-start.12 = (bf16[32,4,4,256]{3,2,1,0:T(4,128)(2,1)S(1)}, bf16[32,4,4,256]{3,2,1,0:T(4,128)(2,1)}, u32[]{:S(2)}) copy-start(bf16[32,4,4,256]{3,2,1,0:T(4,128)(2,1)} %param.18) | copy-start | bytes 786436
  355.8 9.6 %copy-start.1 = (bf16[512,4,256]{2,1,0:T(4,128)(2,1)S(1)}, bf16[512,4,256]{2,1,0:T(4,128)(2,1)}, u32[]{:S(2)}) copy-start(bf16[512,4,256]{2,1,0:T(4,128)(2,1)} %param.14) | copy-start | bytes 3145732
Sparse Core Ops, SparseCore 0:
  15.5 95.3 all-gather.11
  137.7 52.9 all-gather.13
  193.7 107.3 all-gather.7
  303.8 51.9 all-gather.9
where the time goes:
time: 373 us; the launch traced here: 372 us
  waiting for transfers between devices  211 us (57%)
  matrix products  64.5 us (17%)
  other arithmetic  43.6 us (12%)
  blocking collectives  28.4 us (8%)
  between operations  14.7 us (4%)
  local copies, waits for them, and re-layouts  8.8 us (2%)
    all_gather x1, waiting for transfers between devices, shards(): lax.all_gather(retention, 'head', axis=1, tiled=True)  70.3 us
    all_gather x1, waiting for transfers between devices, entering(): pieces = jax.tree.map(lambda part: lax.all_gather(part, axis), value)  66.9 us
    all_gather x1, waiting for transfers between devices, shards(): lax.all_gather(step_flat, 'head', axis=1, tiled=True)  39.1 us
    all_gather x1, waiting for transfers between devices, shards(): lax.all_gather(as_sent(final_state[None]), 'ctx', axis=0, tiled=True)  34.7 us
    unnamed x1, blocking collectives  28.4 us
    dot_general x2, matrix products, project_into(): return jnp.dot(shard_piece, w_out, preferred_element_type=jnp.float32)  24.4 us
    select_n x15, other arithmetic, step(): jnp.where(position < mine, new, old)  23.5 us
    dot_general x2, matrix products, exact_read(): jnp.einsum(form, query_rows, parts[2], preferred_element_type=jnp.float32)  14.3 us
  transfers between devices with their start and end apart: 4, of which 4 were waited for; matrix products, arithmetic and copies ran while one was open for 19% of the time, Pallas kernels for 0%

commit v1 on v0

--- a/solution.py
+++ b/solution.py
@@ -124,7 +124,12 @@
     reads = exact_read(
         "jcthd,jhde->jcthe",
         packed,
-        lax.all_gather(as_sent(final_state[None]), "ctx", axis=0, tiled=True),
+        jnp.concatenate(
+            lax.all_to_all(
+                jnp.stack([as_sent(final_state[None])] * lax.axis_size("ctx")), "ctx", 0, 0
+            ),
+            axis=0,
+        ),
     )
     slot_reads = reads
     slot_reads = slot_reads.reshape(sections * CAP, step_count, heads_here, head_dim)

time: 373 us -> 454 us (1.22)
  waiting for transfers between devices: 211 us -> 293 us
  matrix products: 64.5 us -> 56.1 us
  local copies, waits for them, and re-layouts: 8.8 us -> 14.9 us
  starting transfers between devices: 0.34 us -> 5.49 us
    all_to_all x0 -> x1, waiting for transfers between devices: none -> 90.8 us  [shards(): lax.all_to_all(jnp.stack([as_sent(final_state[None])] * lax.axis_size('ct...]
    all_gather x1 -> x0, waiting for transfers between devices: 34.7 us -> none  [shards(): lax.all_gather(as_sent(final_state[None]), 'ctx', axis=0, tiled=True)]
    all_gather x1, waiting for transfers between devices: 70.3 us -> 98.4 us  [shards(): lax.all_gather(retention, 'head', axis=1, tiled=True)]
    all_to_all x0 -> x1, starting transfers between devices: none -> 5.19 us  [shards(): lax.all_to_all(jnp.stack([as_sent(final_state[None])] * lax.axis_size('ct...]
  transfers between devices with their start and end apart: 4 -> 4, of which waited for: 4 -> 4; matrix products, arithmetic and copies ran while one was open for 19% -> 6% of each run, Pallas kernels for 0% -> 0%
where the time goes in v1:
time: 454 us; the launch traced here: 453 us
  waiting for transfers between devices  293 us (65%)
  matrix products  56.1 us (12%)
  other arithmetic  40.2 us (9%)
  blocking collectives  28.4 us (6%)
  local copies, waits for them, and re-layouts  14.9 us (3%)
  between operations  14.7 us (3%)
  starting transfers between devices  5.49 us (1%)
    all_gather x1, waiting for transfers between devices, shards(): lax.all_gather(retention, 'head', axis=1, tiled=True)  98.4 us
    all_to_all x1, waiting for transfers between devices, shards(): lax.all_to_all(jnp.stack([as_sent(final_state[None])] * lax.axis_size('ct...  90.8 us
    all_gather x1, waiting for transfers between devices, entering(): pieces = jax.tree.map(lambda part: lax.all_gather(part, axis), value)  67 us
    all_gather x1, waiting for transfers between devices, shards(): lax.all_gather(step_flat, 'head', axis=1, tiled=True)  36.6 us
    unnamed x1, blocking collectives  28.4 us
    dot_general x2, matrix products, project_into(): return jnp.dot(shard_piece, w_out, preferred_element_type=jnp.float32)  24.4 us
    select_n x15, other arithmetic, step(): jnp.where(position < mine, new, old)  23.5 us
    convert_element_type x3, other arithmetic, split_state(): middle_part = rest.astype(jnp.bfloat16)  9.77 us
  transfers between devices with their start and end apart: 4, of which 4 were waited for; matrix products, arithmetic and copies ran while one was open for 6% of the time, Pallas kernels for 0%

profile of v1, /device:TPU:1, one launch (start us, length us, event | category | flops | bytes accessed | tf_op | source)
XLA Modules:
  0.0 453.1 jit_solution(10515728223359039443)
XLA Ops:
  7.2 0.8 reshape.129
  8.0 1.2 reduce-window.6
  9.2 0.2 slice_reduce_fusion
  9.4 0.2 reduce-window.9
  9.9 0.2 copy.64
  10.1 1.8 multiply_convert_fusion.1
  11.8 1.2 dynamic-slice
  13.8 1.5 convolution_add_fusion
  15.4 28.4 %all-reduce = f32[64]{0:T(128)S(1)} all-reduce(f32[64]{0:T(128)S(1)} %get-tuple-element.133), channel_id=2, replica_groups=mesh['ctx'=16,'head'=8] {'ctx'}, use_global_device_ids=true, to_apply=%add | all-reduce | flops 64 | bytes 512
  43.9 67.0 %all-gather.10.cloned.1.call-done = f32[64,256,256]{2,1,0:T(8,128)} async-done(((f32[4,256,256]{2,1,0:T(8,128)}), f32[64,256,256]{2,1,0:T(8,128)}) %all-gather.10.cloned.1.call-update) | async-done | bytes 16777232 | tf_op jit(solution)/shard_map/all_gather | solution.py:11
  110.9 24.2 %while.14 = (s32[]{:T(128)}, f32[4,256,256]{2,1,0:T(8,128)S(1)}, s32[]{:T(128)}, f32[16,4]{1,0:T(8,128)S(1)}, f32[16,4,256,256]{3,2,1,0:T(8,128)}, /*index=5*/s32[]{:T(128)}, s32[]{:T(128)}) while((s32[]{:T(128)}, f32[4,256,256]{2,1,0:T(8,128)S(1)}, s32[]{:T(128)}, f32[16,4]{1,0:T(8,128)S(1)}, f32[16,4,256,256]{3,2,1,0:T(8,128)}, ...), condition=%wide.region_3.4_spmd.clone, body=%wide.region_2.3_spmd.clone.sunk | while | flops 1048580 | bytes 3145881 | solution.py:20
  110.9 1.6 fusion.86
  112.6 1.6 fusion.86
  114.2 1.6 fusion.86
  115.8 1.6 fusion.86
  117.4 1.6 fusion.86
  119.1 1.6 fusion.86
  120.7 1.6 fusion.86
  122.3 1.6 fusion.86
  123.9 1.6 fusion.86
  125.5 1.6 fusion.86
  127.1 1.6 fusion.86
  128.7 1.6 fusion.86
  130.3 1.6 fusion.86
  131.9 1.6 fusion.86
  133.5 1.6 fusion.86
  135.1 1.0 add_convert_fusion
  136.1 4.3 stack.2
  140.4 5.2 %all-to-all-start = ((bf16[16,1,4,256,256]{4,3,2,1,0:T(8,128)(2,1)}), bf16[16,1,4,256,256]{4,3,2,1,0:T(8,128)(2,1)}, u32[]{:S(2)}, u32[]{:S(2)}) async-start(bf16[16,1,4,256,256]{4,3,2,1,0:T(8,128)(2,1)} %stack.2), calls=%async_computation | async-start | bytes 16777216 | tf_op jit(solution)/shard_map/all_to_all | solution.py:128
  145.6 0.2 reshape.133
  145.9 0.2 fusion.24
  146.1 0.3 convolution_convert_fusion
  146.4 0.4 reshape.134
  146.8 0.1 copy.73
  147.1 0.5 iota_compare_fusion.7
  147.6 1.2 and_bitcast_fusion
  148.8 0.6 pad_clamp_fusion
  149.4 90.8 %all-to-all-done = bf16[16,1,4,256,256]{4,3,2,1,0:T(8,128)(2,1)} async-done(((bf16[16,1,4,256,256]{4,3,2,1,0:T(8,128)(2,1)}), bf16[16,1,4,256,256]{4,3,2,1,0:T(8,128)(2,1)}, u32[]{:S(2)}, u32[]{:S(2)}) %all-to-all-start) | async-done | bytes 8388640 | tf_op jit(solution)/shard_map/all_to_all | solution.py:128
  240.2 8.4 %fusion.1 = bf16[16,4,256,256]{3,2,1,0:T(8,128)(2,1)S(1)} fusion(bf16[16,4,256,256]{3,2,1,0:T(8,128)(2,1)} %bitcast.13, bf16[16,1,4,256,256]{4,3,2,1,0:T(8,128)(2,1)} %all-to-all-done), kind=kLoop, calls=%fused_computation.6 | loop fusion | flops 16777216 | bytes 25165824 | tf_op jit(solution)/shard_map/convert_element_type | solution.py:30
  248.6 1.4 fusion.3
  250.0 7.9 %fusion.7 = f32[16,4,256,4,4]{2,4,3,1,0:T(4,128)S(1)} fusion(bf16[16,4,256,256]{3,2,1,0:T(8,128)(2,1)S(1)} %fusion.1, bf16[16,4,256,256]{3,2,1,0:T(8,128)(2,1)} %bitcast.13, bf16[16,4,4,4,256]{4,3,2,1,0:T(4,128)(2,1)S(1)} %reshape.134, bf16[16,1,4,256,256]{4,3,2,1,0:T(8,128)(2,1)} %all-to-all-done), kind=kOutput, calls=%fused_computation.12 | convolution fusion | flops 159383552 | bytes 26738688 | tf_op jit(solution)/shard_map/jcthd,jhde->jcthe/dot_general | solution.py:41
  257.9 4.7 %fusion.19 = f32[16,4,4,4,256]{4,2,1,3,0:T(4,128)S(1)} fusion(f32[16,4,256,4,4]{2,4,3,1,0:T(4,128)S(1)} %fusion.7, f32[16,4,256,4,4]{2,4,3,1,0:T(4,128)S(1)} %fusion.3, bf16[16,1,4,256,256]{4,3,2,1,0:T(8,128)(2,1)} %all-to-all-done, bf16[16,4,4,4,256]{4,3,2,1,0:T(4,128)(2,1)S(1)} %reshape.134), kind=kOutput, calls=%fused_computation.26 | convolution fusion | flops 134742016 | bytes 12058624 | tf_op jit(solution)/shard_map/jcthd,jhde->jcthe/dot_general | solution.py:39
  262.6 0.7 copy.77
  263.3 1.7 gather_fusion
  265.0 2.5 fusion.23
  267.5 1.1 copy.84
  268.6 0.7 copy.93
  269.4 0.2 all-gather.6.cloned.1.call-start
  269.8 1.8 fusion.43
  271.7 1.8 fusion.41
  273.5 1.8 fusion.32
  275.3 4.7 %fusion.12 = f32[4,512,256]{1,2,0:T(8,128)} fusion(f32[4,512]{1,0:T(4,128)S(1)} %bitcast.111, pred[512,512]{1,0:T(8,128)(4,1)S(1)} %iota_compare_fusion, bf16[512,4,256]{2,1,0:T(4,128)(2,1)} %param.13, bf16[512,4,256]{2,1,0:T(4,128)(2,1)S(1)} %copy-done, bf16[512,4,256]{2,1,0:T(4,128)(2,1)S(1)} %copy-done.1), kind=kOutput, calls=%fused_computation.22 | convolution fusion | flops 1078984704 | bytes 5513216 | tf_op jit(solution)/shard_map/hnm,mhe->nhe/dot_general | solution.py:55
  279.9 1.3 fusion.31
  281.3 0.5 fusion.36
  281.8 0.5 fusion.38
  282.3 0.7 copy-done.2
  283.0 0.6 copy-done.3
  283.6 0.6 copy-done.4
  284.2 2.1 fusion.10
  286.4 36.6 %all-gather.8.cloned.1.call-done = bf16[128,8192]{1,0:T(8,128)(2,1)} async-done(((bf16[128,1024]{1,0:T(8,128)(2,1)}), bf16[128,8192]{1,0:T(8,128)(2,1)}) %all-gather.8.cloned.1.call-update) | async-done | bytes 2097168 | tf_op jit(solution)/shard_map/all_gather | solution.py:156
  322.9 8.7 %convolution_convert_fusion.2 = bf16[128,1024]{1,0:T(8,128)(2,1)S(1)} fusion(bf16[128,8192]{1,0:T(8,128)(2,1)} %all-gather.8.cloned.1.call-done, bf16[8192,1024]{1,0:T(8,128)(2,1)} %param.21), kind=kOutput, calls=%fused_computation.30 | convolution fusion | flops 2147614720 | bytes 19136512 | tf_op jit(solution)/shard_map/dot_general | solution.py:109
  331.7 0.8 reshape.137
  332.5 98.4 %all-gather.6.cloned.1.call-done = bf16[512,8192]{0,1:T(8,128)(2,1)} async-done(((bf16[512,1024]{0,1:T(8,128)(2,1)}), bf16[512,8192]{0,1:T(8,128)(2,1)}) %all-gather.6.cloned.1.call-update) | async-done | bytes 8388624 | tf_op jit(solution)/shard_map/all_gather | solution.py:111
  430.9 15.7 %convolution_convert_fusion.1 = bf16[512,1024]{1,0:T(8,128)(2,1)} fusion(bf16[512,8192]{0,1:T(8,128)(2,1)} %all-gather.6.cloned.1.call-done, bf16[8192,1024]{1,0:T(8,128)(2,1)} %param.21), kind=kOutput, calls=%fused_computation.21 | convolution fusion | flops 8590458880 | bytes 26214400 | tf_op jit(solution)/shard_map/dot_general | solution.py:109
  (58 shorter events, 1.2 us)
Async XLA Ops:
  7.2 6.7 %copy-start = (bf16[512,4,256]{2,1,0:T(4,128)(2,1)S(1)}, bf16[512,4,256]{2,1,0:T(4,128)(2,1)}, u32[]{:S(2)}) copy-start(bf16[512,4,256]{2,1,0:T(4,128)(2,1)} %param.14) | copy-start | bytes 3145732
  7.2 103.7 %all-gather.10.cloned.1.call-start = ((), (), s32[]{:S(2)}) async-start(), calls=%async_computation.3 | async-start | bytes 17825792 | tf_op jit(solution)/shard_map/all_gather | solution.py:11
  110.9 24.2 %copy-start.6 = (f32[4,256,256]{2,1,0:T(8,128)S(1)}, f32[4,256,256]{2,1,0:T(8,128)}, u32[]{:S(2)}) copy-start(f32[4,256,256]{2,1,0:T(8,128)} %convolution_add_fusion) | copy-start | bytes 3145732
  140.4 5.2 %copy-start.8 = (bf16[32,4,4,256]{3,2,1,0:T(4,128)(2,1)S(1)}, bf16[32,4,4,256]{3,2,1,0:T(4,128)(2,1)}, u32[]{:S(2)}) copy-start(bf16[32,4,4,256]{3,2,1,0:T(4,128)(2,1)} %param.17) | copy-start | bytes 786436
  140.4 5.4 %copy-start.10 = (s32[32,1]{0,1:T(1,128)S(1)}, s32[32,1]{0,1:T(1,128)}, u32[]{:S(2)}) copy-start(s32[32,1]{0,1:T(1,128)} %param.16) | copy-start | bytes 388
  140.4 6.4 %copy-start.9 = (f32[4,4,32]{2,1,0:T(4,128)S(1)}, f32[4,4,32]{2,1,0:T(4,128)}, u32[]{:S(2)}) copy-start(f32[4,4,32]{2,1,0:T(4,128)} %param.20) | copy-start | bytes 6148
  140.4 99.8 %all-to-all-start = ((bf16[16,1,4,256,256]{4,3,2,1,0:T(8,128)(2,1)}), bf16[16,1,4,256,256]{4,3,2,1,0:T(8,128)(2,1)}, u32[]{:S(2)}, u32[]{:S(2)}) async-start(bf16[16,1,4,256,256]{4,3,2,1,0:T(8,128)(2,1)} %stack.2), calls=%async_computation | async-start | bytes 16777216 | tf_op jit(solution)/shard_map/all_to_all | solution.py:128
  145.6 177.3 %all-gather.8.cloned.1.call-start = ((), (), s32[]{:S(2)}) async-start(), calls=%async_computation.2 | async-start | bytes 2359296 | tf_op jit(solution)/shard_map/all_gather | solution.py:156
  146.1 0.7 copy-start.11
  265.0 4.8 %copy-start.1 = (bf16[512,4,256]{2,1,0:T(4,128)(2,1)S(1)}, bf16[512,4,256]{2,1,0:T(4,128)(2,1)}, u32[]{:S(2)}) copy-start(bf16[512,4,256]{2,1,0:T(4,128)(2,1)} %param.12) | copy-start | bytes 3145732
  269.4 161.6 %all-gather.6.cloned.1.call-start = ((), (), s32[]{:S(2)}) async-start(), calls=%async_computation.1 | async-start | bytes 9437184 | tf_op jit(solution)/shard_map/all_gather | solution.py:111
  279.9 1.9 copy-start.5
  279.9 2.4 copy-start.7
  281.2 1.7 copy-start.2
  281.3 2.4 copy-start.3
  281.3 3.0 copy-start.4
Sparse Core Ops, SparseCore 0:
  15.5 95.3 all-gather.9
  269.5 53.4 all-gather.7
  325.9 105.0 all-gather.5
